TPU v7x, 256 devices: a whole 4x4x8 slice. The times are simulated.
256 devices in a mesh: leaf: 64 (over x, z, core), front: 4 (over y).
Axes of the slice: x: 4, y: 4, z: 8, core: 2. Of those that a mesh axis runs over, the one named last changes fastest.
Arguments:
- child_update: bfloat16 [64, 4, 1, 3, 256, 3072], P('leaf', 'front'), may hold values from -60 to 60, as said below
- sep_one: bfloat16 [64, 4, 1, 4, 256, 512], P('leaf', 'front'), may hold values from -60 to 60, as said below
- sep_two: bfloat16 [64, 4, 1, 4, 256, 256], P('leaf', 'front'), may hold values from -60 to 60, as said below
- map_one: int32 [64, 1, 4, 3], replicated, may hold values from 0 to 3, as said below
- map_two: int32 [32, 1, 4, 3], replicated, may hold values from 0 to 3, as said below
- mask_one: int32 [32, 1, 12, 4], replicated, may hold values 0 or 1
- mask_two: int32 [16, 1, 12, 4], replicated, may hold values 0 or 1
Outputs:
- factor_one: float32 [64, 4, 1, 4, 256, 512], P('leaf', 'front')
- factor_two: float32 [64, 4, 1, 4, 256, 256], P('leaf', 'front')
- update_two: bfloat16 [64, 4, 1, 3, 256, 768], P('leaf', 'front')
Inputs may be any that keep to these rules, and one draw needn't show every extreme that they name: `child_update`: every child[l,b] is symmetric positive definite. `sep_one`: the top 1024 rows of each front's initial entries form a symmetric positive definite block, and every assembled front is positive definite. `sep_two`: the top 1024 rows of each front's initial entries form a symmetric positive definite block, and every assembled front is positive definite. `map_one`: for each child, batch and j the 3 entries are distinct; the two children 2p and 2p + 1 leave out different slots, so every parent tile receives one or two child tiles. `map_two`: for each first-level front, batch and j the 3 entries are distinct; fronts 2q and 2q + 1 leave out different slots, so every parent tile receives one or two child tiles.
All inputs are finite; a program needn't handle non-finite values.
Results may differ from a plain program's by a relative error of at most 0.0047.
Values may be sent and summed in bfloat16 or wider, within the bound.
A program may use at most 192 MiB of HBM per device.

v0:
```python
import jax
import jax.numpy as jnp
from jax import lax
from jax.sharding import PartitionSpec as P

TILE = 256
ST = 4
UT = 12
FT = 16
S = 1024
U = 3072
F = 4096


def swapped(value, axis, apart):
    mask = 2**apart
    pairs = [(source, source ^ mask) for source in range(lax.axis_size(axis))]
    return lax.ppermute(value, axis, pairs)


def place_tiles(blocks, row_source, row_live, col_source, col_live):
    taken = jnp.take(blocks, row_source, axis=0)
    taken = jnp.take(taken, col_source, axis=2)
    keep = jnp.logical_and(row_live[:, None, None, None], col_live[None, None, :, None])
    return jnp.where(keep, taken.astype(jnp.float32), 0.0)


def place_child(child_rows, tile_map, column):
    batch_count = child_rows.shape[0]
    local_tiles = child_rows.shape[1]
    groups = tile_map.shape[1]
    slot_count = FT // groups
    own_slots = lax.dynamic_index_in_dim(tile_map, column, 1, keepdims=False)
    row_hit = own_slots[..., None] == jnp.arange(slot_count, dtype=jnp.int32)
    row_source = jnp.sum(
        row_hit.astype(jnp.int32) * jnp.arange(local_tiles, dtype=jnp.int32)[None, :, None], axis=1
    )
    row_live = jnp.any(row_hit, axis=1)
    targets = (jnp.swapaxes(tile_map, 1, 2) * groups + jnp.arange(groups, dtype=jnp.int32)).reshape(
        batch_count, UT
    )
    col_hit = targets[..., None] == jnp.arange(FT, dtype=jnp.int32)
    col_source = jnp.sum(
        col_hit.astype(jnp.int32) * jnp.arange(UT, dtype=jnp.int32)[None, :, None], axis=1
    )
    col_live = jnp.any(col_hit, axis=1)
    blocks = child_rows.reshape(batch_count, local_tiles, TILE, UT, TILE)
    placed = jax.vmap(place_tiles)(blocks, row_source, row_live, col_source, col_live)
    return placed.reshape(batch_count, slot_count, TILE, F)


def join_halves(mine, other, position):
    lower_first = jnp.concatenate([mine, other], axis=-1)
    upper_first = jnp.concatenate([other, mine], axis=-1)
    return jnp.where(position == 0, lower_first, upper_first)


def add_initial(canvas, initial, mask_front, column):
    batch_count = canvas.shape[0]
    slot_count = canvas.shape[1]
    groups = lax.axis_size("front")
    mask_rows = mask_front.reshape(batch_count, slot_count - 1, groups, ST)
    mask_rows = lax.dynamic_index_in_dim(mask_rows, column, 2, keepdims=False).astype(jnp.float32)
    mask_all = jnp.concatenate([jnp.ones((batch_count, 1, ST), jnp.float32), mask_rows], axis=1)
    weighted = initial.astype(jnp.float32).reshape(batch_count, slot_count, TILE, ST, TILE)
    weighted = (weighted * mask_all[:, :, None, :, None]).reshape(batch_count, slot_count, TILE, S)
    return jnp.concatenate([canvas[:, :, :, :S] + weighted, canvas[:, :, :, S:]], axis=-1)


def factor_front(canvas, column):
    batch_count = canvas.shape[0]
    local_tiles = canvas.shape[1] - 1
    groups = lax.axis_size("front")
    pivot_piece = canvas[:, :1, :, :S]
    pivot_all = lax.all_gather(pivot_piece[None], "front", axis=0, tiled=True)
    pivot_block = jnp.moveaxis(pivot_all, 0, 2).reshape(batch_count, S, S)
    lower_factor = jnp.linalg.cholesky(pivot_block)
    coupling = canvas[:, 1:, :, :S].reshape(batch_count, local_tiles * TILE, S)
    panel_full = lax.linalg.triangular_solve(
        lower_factor, coupling, left_side=False, lower=True, transpose_a=True
    )
    panel_round = panel_full.astype(jnp.bfloat16)
    shared = lax.all_gather(
        panel_round.reshape(batch_count, local_tiles, TILE, S)[None], "front", axis=0, tiled=True
    )
    ordered = jnp.transpose(shared, (1, 2, 0, 3, 4)).reshape(batch_count, U, S)
    own_lower = lax.dynamic_index_in_dim(
        lower_factor.reshape(batch_count, groups, TILE, S), column, 1, keepdims=True
    )
    factor_rows = jnp.concatenate(
        [own_lower, panel_full.reshape(batch_count, local_tiles, TILE, S)], axis=1
    )
    trailing = canvas[:, 1:, :, S:].reshape(batch_count, local_tiles * TILE, U)
    product = jnp.einsum("brk,bnk->brn", panel_round, ordered, preferred_element_type=jnp.float32)
    update = (trailing - product).astype(jnp.bfloat16)
    return (factor_rows, update)


def body(child_update, sep_one, sep_two, map_one, map_two, mask_one, mask_two):
    column = lax.axis_index("front")
    leaf_index = lax.axis_index("leaf")
    half_index = leaf_index % 2
    quarter_index = leaf_index % 4
    pair_index = leaf_index // 2
    quad_index = leaf_index // 4
    side_index = pair_index % 2
    child_rows = child_update[0, 0]
    batch_count = child_rows.shape[0]
    local_tiles = child_rows.shape[1]
    entries_one = sep_one[0, 0]
    entries_two = sep_two[0, 0]
    peer_rows, peer_one, peer_two = swapped((child_rows, entries_one, entries_two), "leaf", 0)
    map_own = lax.dynamic_index_in_dim(map_one, leaf_index, 0, keepdims=False)
    map_peer = lax.dynamic_index_in_dim(map_one, jnp.bitwise_xor(leaf_index, 1), 0, keepdims=False)
    front_first = place_child(child_rows, map_own, column) + place_child(
        peer_rows, map_peer, column
    )
    initial_one = join_halves(entries_one, peer_one, half_index)
    mask_front = lax.dynamic_index_in_dim(mask_one, pair_index, 0, keepdims=False)
    front_first = add_initial(front_first, initial_one, mask_front, column)
    factor_rows_one, update_one = factor_front(front_first, column)
    factor_one = lax.dynamic_slice_in_dim(factor_rows_one, half_index * (S // 2), S // 2, 3)
    entries_half = join_halves(entries_two, peer_two, quarter_index % 2)
    update_far, entries_far = swapped((update_one, entries_half), "leaf", 1)
    map_near = lax.dynamic_index_in_dim(map_two, pair_index, 0, keepdims=False)
    map_far = lax.dynamic_index_in_dim(map_two, jnp.bitwise_xor(pair_index, 1), 0, keepdims=False)
    near_rows = update_one.reshape(batch_count, local_tiles, TILE, U)
    far_rows = update_far.reshape(batch_count, local_tiles, TILE, U)
    front_second = place_child(near_rows, map_near, column) + place_child(far_rows, map_far, column)
    initial_two = join_halves(entries_half, entries_far, side_index)
    mask_second = lax.dynamic_index_in_dim(mask_two, quad_index, 0, keepdims=False)
    front_second = add_initial(front_second, initial_two, mask_second, column)
    factor_rows_two, update_last = factor_front(front_second, column)
    update_last = lax.dynamic_slice_in_dim(update_last, quarter_index * (U // 4), U // 4, 2)
    factor_two = lax.dynamic_slice_in_dim(factor_rows_two, quarter_index * (S // 4), S // 4, 3)
    update_two = update_last.reshape(batch_count, local_tiles, TILE, U // 4)
    return (factor_one[None, None], factor_two[None, None], update_two[None, None])


def solution(mesh):
    return jax.shard_map(
        body,
        mesh=mesh,
        in_specs=(
            P("leaf", "front", None, None, None, None),
            P("leaf", "front", None, None, None, None),
            P("leaf", "front", None, None, None, None),
            P(),
            P(),
            P(),
            P(),
        ),
        out_specs=(
            P("leaf", "front", None, None, None, None),
            P("leaf", "front", None, None, None, None),
            P("leaf", "front", None, None, None, None),
        ),
        check_vma=False,
    )
```

profile of v0, /device:TPU:1, one launch (start us, length us, event | category | flops | bytes accessed | tf_op | source)
XLA Modules:
  0.0 1299.8 jit_solution(7646188197757473696)
XLA Ops:
  74.5 13.8 %select_add_fusion.1 = f32[1,4,256,16,256]{4,2,1,3,0:T(8,128)} fusion(bf16[16,4,256,256]{3,2,1,0:T(8,128)(2,1)} %gather_fusion.3, bf16[16,4,256,256]{3,2,1,0:T(8,128)(2,1)} %gather_fusion.1, pred[16]{0:T(512)(128)(4,1)S(1)} %and_bitcast_fusion.4, pred[16]{0:T(512)(128)(4,1)S(1)} %and_bitcast_fusion.6, pred[4,16]{0,1:T(8,128)(4,1)S(1)} %broadcast_and_fusion.2, ...), kind=kLoop, calls=%fused_computation.13 | loop fusion | flops 29360128 | bytes 33554592 | tf_op jit(solution)/shard_map/add | solution.py:115
  88.3 16.4 %copy.145 = f32[1,4,256,16,256]{2,4,3,1,0:T(8,128)} copy(f32[1,4,256,16,256]{4,2,1,3,0:T(8,128)} %select_add_fusion.1) | data formatting | bytes 33554432 | tf_op jit(solution)/shard_map/add | solution.py:115
  116.7 47.7 %all-gather.11.cloned.1.call-done = f32[4,1,256,1024]{3,2,1,0:T(8,128)} async-done(((f32[1,1,256,1024]{3,2,1,0:T(8,128)}), f32[4,1,256,1024]{3,2,1,0:T(8,128)}) %all-gather.11.cloned.1.call-update) | async-done | bytes 4194320 | tf_op jit(solution)/shard_map/all_gather | solution.py:75
  176.6 11.7 custom-call.91
  205.2 11.9 custom-call.93
  231.5 11.7 custom-call.95
  257.9 11.9 custom-call.97
  284.4 11.7 custom-call.99
  297.5 10.2 custom-call.100
  311.0 11.7 custom-call.101
  336.8 11.9 custom-call.103
  362.3 11.7 custom-call.105
  387.9 28.1 %while.4 = (s32[]{:T(128)}, f32[1,1024,1024]{2,1,0:T(8,128)}, s32[8,2]{0,1:T(2,128)S(1)}, f32[8,1,128,128]{3,2,1,0:T(8,128)}, s32[]{:T(128)}) while((s32[]{:T(128)}, f32[1,1024,1024]{2,1,0:T(8,128)}, s32[8,2]{0,1:T(2,128)S(1)}, f32[8,1,128,128]{3,2,1,0:T(8,128)}, s32[]{:T(128)}) %tuple.131), condition=%wide.while_cond, body=%wide.while_body.sunk | while | flops 2 | bytes 132205 | solution.py:79
  416.0 80.4 %custom-call.106 = f32[1,8,128,128]{2,3,1,0:T(8,128)} custom-call(f32[1,8,128,128]{3,2,1,0:T(8,128)} %bitcast.928), custom_call_target="InvertDiagBlocksLowerTriangular" | custom-call | tf_op jit(solution)/shard_map/triangular_solve/custom-call.7 | solution.py:79
  549.6 50.9 %all-gather.7.cloned.1.call-done = bf16[4,1,3,256,1024]{4,3,2,1,0:T(8,128)(2,1)} async-done(((bf16[1,1,3,256,1024]{4,3,2,1,0:T(8,128)(2,1)}), bf16[4,1,3,256,1024]{4,3,2,1,0:T(8,128)(2,1)}) %all-gather.7.cloned.1.call-update) | async-done | bytes 6291472 | tf_op jit(solution)/shard_map/all_gather | solution.py:83
  654.7 61.9 %collective-permute-done.2 = bf16[1,768,3072]{2,1,0:T(8,128)(2,1)} collective-permute-done((bf16[1,768,3072]{2,1,0:T(8,128)(2,1)}, bf16[1,768,3072]{2,1,0:T(8,128)(2,1)}, u32[]{:S(2)}, u32[]{:S(2)}) %collective-permute-start.2) | collective-permute-done | bytes 4718624 | tf_op jit(solution)/shard_map/ppermute | solution.py:18
  752.2 13.8 %select_add_fusion = f32[1,4,256,16,256]{4,2,1,3,0:T(8,128)} fusion(bf16[16,4,256,256]{3,2,1,0:T(8,128)(2,1)} %gather_fusion.7, bf16[16,4,256,256]{3,2,1,0:T(8,128)(2,1)} %gather_fusion.5, pred[16]{0:T(512)(128)(4,1)S(1)} %and_bitcast_fusion, pred[16]{0:T(512)(128)(4,1)S(1)} %and_bitcast_fusion.2, pred[4,16]{0,1:T(8,128)(4,1)S(1)} %broadcast_and_fusion, ...), kind=kLoop, calls=%fused_computation.12 | loop fusion | flops 29360128 | bytes 33554592 | tf_op jit(solution)/shard_map/add | solution.py:129
  766.0 16.4 %copy.163 = f32[1,4,256,16,256]{2,4,3,1,0:T(8,128)} copy(f32[1,4,256,16,256]{4,2,1,3,0:T(8,128)} %select_add_fusion) | data formatting | bytes 33554432 | tf_op jit(solution)/shard_map/add | solution.py:129
  793.6 49.4 %all-gather.13.cloned.1.call-done = f32[4,1,256,1024]{3,2,1,0:T(8,128)} async-done(((f32[1,1,256,1024]{3,2,1,0:T(8,128)}), f32[4,1,256,1024]{3,2,1,0:T(8,128)}) %all-gather.13.cloned.1.call-update) | async-done | bytes 4194320 | tf_op jit(solution)/shard_map/all_gather | solution.py:75
  854.9 11.7 custom-call.111
  883.5 11.9 custom-call.113
  909.9 11.7 custom-call.115
  936.2 12.1 custom-call.117
  962.9 11.7 custom-call.119
  975.9 9.9 custom-call.120
  989.2 11.7 custom-call.121
  1015.0 11.9 custom-call.123
  1040.6 11.7 custom-call.125
  1066.2 28.1 %while.5 = (s32[]{:T(128)}, f32[1,1024,1024]{2,1,0:T(8,128)}, s32[8,2]{0,1:T(2,128)S(1)}, f32[8,1,128,128]{3,2,1,0:T(8,128)}, s32[]{:T(128)}) while((s32[]{:T(128)}, f32[1,1024,1024]{2,1,0:T(8,128)}, s32[8,2]{0,1:T(2,128)S(1)}, f32[8,1,128,128]{3,2,1,0:T(8,128)}, s32[]{:T(128)}) %tuple.145), condition=%wide.while_cond.clone, body=%wide.while_body.clone.sunk | while | flops 2 | bytes 132205 | solution.py:79
  1094.3 80.4 %custom-call.126 = f32[1,8,128,128]{2,3,1,0:T(8,128)} custom-call(f32[1,8,128,128]{3,2,1,0:T(8,128)} %bitcast.927), custom_call_target="InvertDiagBlocksLowerTriangular" | custom-call | tf_op jit(solution)/shard_map/triangular_solve/custom-call.7 | solution.py:79
  1227.9 10.1 copy.173
  1244.0 37.3 %all-gather.9.cloned.1.call-done = bf16[4,1,3,256,1024]{4,3,2,1,0:T(8,128)(2,1)} async-done(((bf16[1,1,3,256,1024]{4,3,2,1,0:T(8,128)(2,1)}), bf16[4,1,3,256,1024]{4,3,2,1,0:T(8,128)(2,1)}) %all-gather.9.cloned.1.call-update) | async-done | bytes 6291472 | tf_op jit(solution)/shard_map/all_gather | solution.py:83
  (354 shorter events, 587.5 us)
Async XLA Ops:
  7.2 11.9 copy-start
  7.2 157.2 %all-gather.11.cloned.1.call-start = ((), (), s32[]{:S(2)}) async-start(), calls=%async_computation.2 | async-start | bytes 5242880 | tf_op jit(solution)/shard_map/all_gather | solution.py:75
  8.7 10.0 copy-start.18
  8.7 10.8 copy-start.19
  8.7 11.2 copy-start.17
  8.7 95.9 %collective-permute-start.1 = (bf16[1,4,256,512]{2,3,1,0:T(8,128)(2,1)S(1)}, bf16[1,4,256,512]{2,3,1,0:T(8,128)(2,1)S(1)}, u32[]{:S(2)}, u32[]{:S(2)}) collective-permute-start(bf16[1,4,256,512]{2,3,1,0:T(8,128)(2,1)S(1)} %bitcast.921), channel_id=1, source_target_pairs={{0,4},{4,0},{8,12},{12,8},{16,20},{20,16},{24,28},{28,24},{32,36},... | collective-permute-start | bytes 3145736 | tf_op jit(solution)/shard_map/ppermute | solution.py:18
  18.7 29.6 %collective-permute-start = (bf16[1,3,256,3072]{2,3,1,0:T(8,128)(2,1)}, bf16[1,3,256,3072]{2,3,1,0:T(8,128)(2,1)}, u32[]{:S(2)}, u32[]{:S(2)}) collective-permute-start(bf16[1,3,256,3072]{2,3,1,0:T(8,128)(2,1)} %bitcast.880), channel_id=1, source_target_pairs={{0,4},{4,0},{8,12},{12,8},{16,20},{20,16},{24,28},{28,24},{32,36},... | collective-permute-start | bytes 14155784 | tf_op jit(solution)/shard_map/ppermute | solution.py:18
  109.0 2.0 copy-start.2
  112.3 1.9 slice-start
  112.4 488.2 %all-gather.7.cloned.1.call-start = ((), (), s32[]{:S(2)}) async-start(), calls=%async_computation | async-start | bytes 7864320 | tf_op jit(solution)/shard_map/all_gather | solution.py:83
  174.6 1.9 copy-start.10
  380.3 116.2 %copy-start.9 = (f32[1,3,256,1024]{3,2,1,0:T(8,128)S(1)}, f32[1,3,256,1024]{3,2,1,0:T(8,128)}, u32[]{:S(2)}) copy-start(f32[1,3,256,1024]{3,2,1,0:T(8,128)} %copy.152) | copy-start | bytes 9437188
  496.4 6.9 copy-start.14
  528.4 1.7 copy-start.4
  531.8 311.2 %all-gather.13.cloned.1.call-start = ((), (), s32[]{:S(2)}) async-start(), calls=%async_computation.3 | async-start | bytes 5242880 | tf_op jit(solution)/shard_map/all_gather | solution.py:75
  600.5 5.5 copy-start.12
  606.0 8.9 copy-start.16
  613.7 102.9 %collective-permute-start.2 = (bf16[1,768,3072]{2,1,0:T(8,128)(2,1)}, bf16[1,768,3072]{2,1,0:T(8,128)(2,1)}, u32[]{:S(2)}, u32[]{:S(2)}) collective-permute-start(bf16[1,768,3072]{2,1,0:T(8,128)(2,1)} %bitcast.920), channel_id=1, source_target_pairs={{0,8},{4,12},{8,0},{12,4},{16,24},{20,28},{24,16},{28,20},{32,40},... | collective-permute-start | bytes 14155784 | tf_op jit(solution)/shard_map/ppermute | solution.py:18
  615.2 2.6 collective-permute-start.3
  618.0 164.3 %collective-permute-start.4 = (bf16[1,4,256,512]{2,3,1,0:T(8,128)(2,1)S(1)}, bf16[1,4,256,512]{2,3,1,0:T(8,128)(2,1)}, u32[]{:S(2)}, u32[]{:S(2)}) collective-permute-start(bf16[1,4,256,512]{2,3,1,0:T(8,128)(2,1)S(1)} %maximum_select_fusion.3), channel_id=1, source_target_pairs={{0,8},{4,12},{8,0},{12,4},{16,24},{20,28},{24,16},{28,20},{32,40},... | collective-permute-start | bytes 3145736 | tf_op jit(solution)/shard_map/ppermute | solution.py:18
  785.9 2.0 copy-start.3
  789.3 1.9 slice-start.1
  789.3 492.0 %all-gather.9.cloned.1.call-start = ((), (), s32[]{:S(2)}) async-start(), calls=%async_computation.1 | async-start | bytes 7864320 | tf_op jit(solution)/shard_map/all_gather | solution.py:83
  853.0 1.9 copy-start.11
  1058.6 116.1 %copy-start.8 = (f32[1,3,256,1024]{3,2,1,0:T(8,128)S(1)}, f32[1,3,256,1024]{3,2,1,0:T(8,128)}, u32[]{:S(2)}) copy-start(f32[1,3,256,1024]{3,2,1,0:T(8,128)} %copy.171) | copy-start | bytes 9437188
  1174.7 6.9 copy-start.15
  1206.7 1.7 copy-start.6
  1208.4 4.1 copy-start.5
  1227.9 10.1 copy-start.7
  1244.0 40.8 %copy-start.13 = (bf16[1,768,1024]{1,2,0:T(8,128)(2,1)S(1)}, bf16[1,768,1024]{1,2,0:T(8,128)(2,1)}, u32[]{:S(2)}) copy-start(bf16[1,768,1024]{1,2,0:T(8,128)(2,1)} %convert_element_type.105) | copy-start | bytes 4718596
  1284.8 8.2 copy-start.1
Sparse Core Ops, SparseCore 0:
  112.5 51.8 all-gather.10
  532.0 68.5 all-gather.6
  789.4 53.5 all-gather.12
  1212.7 68.5 all-gather.8
where the time goes:
time: 1310 us; the launch traced here: 1300 us
  other arithmetic  602 us (46%)
  local copies, waits for them, and re-layouts  297 us (23%)
  waiting for transfers between devices  248 us (19%)
  matrix products  123 us (9%)
  between operations  25 us (2%)
    another operation x62, other arithmetic, factor_front(): lower_factor = jnp.linalg.cholesky(pivot_block)  346 us
    another operation x5, other arithmetic, factor_front(): lax.linalg.triangular_solve(lower_factor, coupling, left_side=False, lowe...  174 us
    all_gather x2, waiting for transfers between devices, factor_front(): pivot_all = lax.all_gather(pivot_piece[None], 'front', axis=0, tiled=True)  97.1 us
    all_gather x2, waiting for transfers between devices, factor_front(): lax.all_gather(panel_round.reshape(batch_count, local_tiles, TILE, S)[Non...  88.2 us
    another operation x30, matrix products, factor_front(): lax.linalg.triangular_solve(lower_factor, coupling, left_side=False, lowe...  63.6 us
    another operation x53, local copies, waits for them, and re-layouts, factor_front(): lax.linalg.triangular_solve(lower_factor, coupling, left_side=False, lowe...  62.7 us
    ppermute x5, waiting for transfers between devices, swapped(): return lax.ppermute(value, axis, pairs)  62.4 us
    another operation x28, matrix products, factor_front(): lower_factor = jnp.linalg.cholesky(pivot_block)  46.3 us
  transfers between devices with their start and end apart: 9, of which 6 were waited for; matrix products, arithmetic and copies ran while one was open for 19% of the time, Pallas kernels for 0%

commit v1 on v0

--- a/solution.py
+++ b/solution.py
@@ -10,6 +10,19 @@
 S = 1024
 U = 3072
 F = 4096
+
+
+def ring_gather(shard, axis, dim):
+    ways = lax.axis_size(axis)
+    up = [(d, (d + 1) % ways) for d in range(ways)]
+    down = [(d, (d - 1) % ways) for d in range(ways)]
+    earlier, later = ([shard], [shard])
+    for _ in range(ways // 2):
+        earlier.append(lax.ppermute(earlier[-1], axis, up))
+    for _ in range((ways - 1) // 2):
+        later.append(lax.ppermute(later[-1], axis, down))
+    line = jnp.concatenate([*earlier[::-1], *later[1:]], axis=dim)
+    return jnp.roll(line, (lax.axis_index(axis) - ways // 2) * shard.shape[dim], axis=dim)
 
 
 def swapped(value, axis, apart):
@@ -72,7 +85,7 @@
     local_tiles = canvas.shape[1] - 1
     groups = lax.axis_size("front")
     pivot_piece = canvas[:, :1, :, :S]
-    pivot_all = lax.all_gather(pivot_piece[None], "front", axis=0, tiled=True)
+    pivot_all = ring_gather(pivot_piece[None], "front", 0)
     pivot_block = jnp.moveaxis(pivot_all, 0, 2).reshape(batch_count, S, S)
     lower_factor = jnp.linalg.cholesky(pivot_block)
     coupling = canvas[:, 1:, :, :S].reshape(batch_count, local_tiles * TILE, S)

time: 1310 us -> 1340 us (1.023)
  local copies, waits for them, and re-layouts: 297 us -> 313 us
    all_gather x2 -> x0, waiting for transfers between devices: 97.1 us -> none  [factor_front(): pivot_all = lax.all_gather(pivot_piece[None], 'front', axis=0, tiled=True)]
    ppermute x0 -> x6, waiting for transfers between devices: none -> 86.2 us  [the longest x4 86.2 us: ring_gather(): earlier.append(lax.ppermute(earlier[-1], axis, up))]
  transfers between devices with their start and end apart: 9 -> 13, of which waited for: 6 -> 7; matrix products, arithmetic and copies ran while one was open for 19% -> 20% of each run, Pallas kernels for 0% -> 0%
where the time goes in v1:
time: 1340 us; the launch traced here: 1320 us
  other arithmetic  614 us (46%)
  local copies, waits for them, and re-layouts  313 us (23%)
  waiting for transfers between devices  237 us (18%)
  matrix products  123 us (9%)
  between operations  25.6 us (2%)
    another operation x62, other arithmetic, factor_front(): lower_factor = jnp.linalg.cholesky(pivot_block)  346 us
    another operation x5, other arithmetic, factor_front(): lax.linalg.triangular_solve(lower_factor, coupling, left_side=False, lowe...  174 us
    all_gather x2, waiting for transfers between devices, factor_front(): lax.all_gather(panel_round.reshape(batch_count, local_tiles, TILE, S)[Non...  87.7 us
    ppermute x4, waiting for transfers between devices, ring_gather(): earlier.append(lax.ppermute(earlier[-1], axis, up))  86.2 us
    another operation x30, matrix products, factor_front(): lax.linalg.triangular_solve(lower_factor, coupling, left_side=False, lowe...  63.6 us
    ppermute x5, waiting for transfers between devices, swapped(): return lax.ppermute(value, axis, pairs)  62.9 us
    another operation x53, local copies, waits for them, and re-layouts, factor_front(): lax.linalg.triangular_solve(lower_factor, coupling, left_side=False, lowe...  62.8 us
    another operation x28, matrix products, factor_front(): lower_factor = jnp.linalg.cholesky(pivot_block)  46.3 us
  transfers between devices with their start and end apart: 13, of which 7 were waited for; matrix products, arithmetic and copies ran while one was open for 20% of the time, Pallas kernels for 0%

profile of v1, /device:TPU:1, one launch (start us, length us, event | category | flops | bytes accessed | tf_op | source)
XLA Modules:
  0.0 1324.9 jit_solution(2814393110744437928)
XLA Ops:
  74.1 13.8 %select_add_fusion.1 = f32[1,4,256,16,256]{4,2,1,3,0:T(8,128)} fusion(bf16[16,4,256,256]{3,2,1,0:T(8,128)(2,1)} %gather_fusion.3, bf16[16,4,256,256]{3,2,1,0:T(8,128)(2,1)} %gather_fusion.1, pred[16]{0:T(512)(128)(4,1)S(1)} %and_bitcast_fusion.4, pred[16]{0:T(512)(128)(4,1)S(1)} %and_bitcast_fusion.6, pred[4,16]{0,1:T(8,128)(4,1)S(1)} %broadcast_and_fusion.2, ...), kind=kLoop, calls=%fused_computation.13 | loop fusion | flops 29360128 | bytes 33554592 | tf_op jit(solution)/shard_map/add | solution.py:128
  87.9 16.4 %copy.141 = f32[1,4,256,16,256]{2,4,3,1,0:T(8,128)} copy(f32[1,4,256,16,256]{4,2,1,3,0:T(8,128)} %select_add_fusion.1) | data formatting | bytes 33554432 | tf_op jit(solution)/shard_map/add | solution.py:128
  114.2 23.1 %collective-permute-done.2 = f32[1,1,1,256,1024]{3,4,2,1,0:T(8,128)} collective-permute-done((f32[1,1,1,256,1024]{3,4,2,1,0:T(8,128)}, f32[1,1,1,256,1024]{3,4,2,1,0:T(8,128)}, u32[]{:S(2)}, u32[]{:S(2)}) %collective-permute-start.2) | collective-permute-done | bytes 1048608 | tf_op jit(solution)/shard_map/ppermute | solution.py:21
  140.0 22.3 %collective-permute-done.3 = f32[1,1,1,256,1024]{3,4,2,1,0:T(8,128)} collective-permute-done((f32[1,1,1,256,1024]{3,4,2,1,0:T(8,128)}, f32[1,1,1,256,1024]{3,4,2,1,0:T(8,128)}, u32[]{:S(2)}, u32[]{:S(2)}) %collective-permute-start.3) | collective-permute-done | bytes 1048608 | tf_op jit(solution)/shard_map/ppermute | solution.py:21
  190.5 11.7 custom-call.91
  219.2 11.9 custom-call.93
  245.5 11.7 custom-call.95
  271.9 11.9 custom-call.97
  298.4 11.7 custom-call.99
  324.9 11.7 custom-call.101
  350.7 11.9 custom-call.103
  376.3 11.7 custom-call.105
  401.8 28.1 %while.4 = (s32[]{:T(128)}, f32[1,1024,1024]{2,1,0:T(8,128)}, s32[8,2]{0,1:T(2,128)S(1)}, f32[8,1,128,128]{3,2,1,0:T(8,128)}, s32[]{:T(128)}) while((s32[]{:T(128)}, f32[1,1024,1024]{2,1,0:T(8,128)}, s32[8,2]{0,1:T(2,128)S(1)}, f32[8,1,128,128]{3,2,1,0:T(8,128)}, s32[]{:T(128)}) %tuple.132), condition=%wide.while_cond, body=%wide.while_body.sunk | while | flops 2 | bytes 132205 | solution.py:92
  429.9 80.4 %custom-call.106 = f32[1,8,128,128]{2,3,1,0:T(8,128)} custom-call(f32[1,8,128,128]{3,2,1,0:T(8,128)} %bitcast.962), custom_call_target="InvertDiagBlocksLowerTriangular" | custom-call | tf_op jit(solution)/shard_map/triangular_solve/custom-call.7 | solution.py:92
  566.9 47.7 %all-gather.3.cloned.1.call-done = bf16[4,1,3,256,1024]{4,3,2,1,0:T(8,128)(2,1)} async-done(((bf16[1,1,3,256,1024]{4,3,2,1,0:T(8,128)(2,1)}), bf16[4,1,3,256,1024]{4,3,2,1,0:T(8,128)(2,1)}) %all-gather.3.cloned.1.call-update) | async-done | bytes 6291472 | tf_op jit(solution)/shard_map/all_gather | solution.py:96
  667.7 62.9 %collective-permute-done.5 = bf16[1,768,3072]{2,1,0:T(8,128)(2,1)} collective-permute-done((bf16[1,768,3072]{2,1,0:T(8,128)(2,1)}, bf16[1,768,3072]{2,1,0:T(8,128)(2,1)}, u32[]{:S(2)}, u32[]{:S(2)}) %collective-permute-start.5) | collective-permute-done | bytes 4718624 | tf_op jit(solution)/shard_map/ppermute | solution.py:31
  766.2 13.8 %select_add_fusion = f32[1,4,256,16,256]{4,2,1,3,0:T(8,128)} fusion(bf16[16,4,256,256]{3,2,1,0:T(8,128)(2,1)} %gather_fusion.7, bf16[16,4,256,256]{3,2,1,0:T(8,128)(2,1)} %gather_fusion.5, pred[16]{0:T(512)(128)(4,1)S(1)} %and_bitcast_fusion, pred[16]{0:T(512)(128)(4,1)S(1)} %and_bitcast_fusion.2, pred[4,16]{0,1:T(8,128)(4,1)S(1)} %broadcast_and_fusion, ...), kind=kLoop, calls=%fused_computation.12 | loop fusion | flops 29360128 | bytes 33554592 | tf_op jit(solution)/shard_map/add | solution.py:142
  780.0 16.4 %copy.158 = f32[1,4,256,16,256]{2,4,3,1,0:T(8,128)} copy(f32[1,4,256,16,256]{4,2,1,3,0:T(8,128)} %select_add_fusion) | data formatting | bytes 33554432 | tf_op jit(solution)/shard_map/add | solution.py:142
  805.7 20.7 %collective-permute-done.8 = f32[1,1,1,256,1024]{3,4,2,1,0:T(8,128)} collective-permute-done((f32[1,1,1,256,1024]{3,4,2,1,0:T(8,128)}, f32[1,1,1,256,1024]{3,4,2,1,0:T(8,128)}, u32[]{:S(2)}, u32[]{:S(2)}) %collective-permute-start.8) | collective-permute-done | bytes 1048608 | tf_op jit(solution)/shard_map/ppermute | solution.py:21
  828.9 20.0 %collective-permute-done.9 = f32[1,1,1,256,1024]{3,4,2,1,0:T(8,128)} collective-permute-done((f32[1,1,1,256,1024]{3,4,2,1,0:T(8,128)}, f32[1,1,1,256,1024]{3,4,2,1,0:T(8,128)}, u32[]{:S(2)}, u32[]{:S(2)}) %collective-permute-start.9) | collective-permute-done | bytes 1048608 | tf_op jit(solution)/shard_map/ppermute | solution.py:21
  876.9 11.7 custom-call.111
  905.6 12.1 custom-call.113
  932.1 11.7 custom-call.115
  958.5 11.9 custom-call.117
  984.9 11.7 custom-call.119
  1011.2 11.7 custom-call.121
  1037.0 12.1 custom-call.123
  1062.9 11.7 custom-call.125
  1088.5 28.1 %while.5 = (s32[]{:T(128)}, f32[1,1024,1024]{2,1,0:T(8,128)}, s32[8,2]{0,1:T(2,128)S(1)}, f32[8,1,128,128]{3,2,1,0:T(8,128)}, s32[]{:T(128)}) while((s32[]{:T(128)}, f32[1,1024,1024]{2,1,0:T(8,128)}, s32[8,2]{0,1:T(2,128)S(1)}, f32[8,1,128,128]{3,2,1,0:T(8,128)}, s32[]{:T(128)}) %tuple.142), condition=%wide.while_cond.clone, body=%wide.while_body.clone.sunk | while | flops 2 | bytes 132205 | solution.py:92
  1116.6 80.2 %custom-call.126 = f32[1,8,128,128]{2,3,1,0:T(8,128)} custom-call(f32[1,8,128,128]{3,2,1,0:T(8,128)} %bitcast.961), custom_call_target="InvertDiagBlocksLowerTriangular" | custom-call | tf_op jit(solution)/shard_map/triangular_solve/custom-call.7 | solution.py:92
  1249.4 10.5 copy.167
  1265.9 40.0 %all-gather.5.cloned.1.call-done = bf16[4,1,3,256,1024]{4,3,2,1,0:T(8,128)(2,1)} async-done(((bf16[1,1,3,256,1024]{4,3,2,1,0:T(8,128)(2,1)}), bf16[4,1,3,256,1024]{4,3,2,1,0:T(8,128)(2,1)}) %all-gather.5.cloned.1.call-update) | async-done | bytes 6291472 | tf_op jit(solution)/shard_map/all_gather | solution.py:96
  (364 shorter events, 642.4 us)
Async XLA Ops:
  7.2 11.6 copy-start
  7.2 607.4 %all-gather.3.cloned.1.call-start = ((), (), s32[]{:S(2)}) async-start(), calls=%async_computation | async-start | bytes 7864320 | tf_op jit(solution)/shard_map/all_gather | solution.py:96
  8.7 10.4 copy-start.19
  8.7 10.8 copy-start.17
  8.7 10.8 copy-start.18
  8.7 95.5 %collective-permute-start.1 = (bf16[1,4,256,512]{2,3,1,0:T(8,128)(2,1)S(1)}, bf16[1,4,256,512]{2,3,1,0:T(8,128)(2,1)S(1)}, u32[]{:S(2)}, u32[]{:S(2)}) collective-permute-start(bf16[1,4,256,512]{2,3,1,0:T(8,128)(2,1)S(1)} %bitcast.955), channel_id=1, source_target_pairs={{0,4},{4,0},{8,12},{12,8},{16,20},{20,16},{24,28},{28,24},{32,36},... | collective-permute-start | bytes 3145736 | tf_op jit(solution)/shard_map/ppermute | solution.py:31
  18.7 29.1 %collective-permute-start = (bf16[1,3,256,3072]{2,3,1,0:T(8,128)(2,1)}, bf16[1,3,256,3072]{2,3,1,0:T(8,128)(2,1)}, u32[]{:S(2)}, u32[]{:S(2)}) collective-permute-start(bf16[1,3,256,3072]{2,3,1,0:T(8,128)(2,1)} %bitcast.918), channel_id=1, source_target_pairs={{0,4},{4,0},{8,12},{12,8},{16,20},{20,16},{24,28},{28,24},{32,36},... | collective-permute-start | bytes 14155784 | tf_op jit(solution)/shard_map/ppermute | solution.py:31
  108.6 1.9 copy-start.2
  111.5 26.0 %slice-start = ((f32[1,4,256,1024]{2,3,1,0:T(8,128)}), f32[1,3,256,1024]{2,3,1,0:T(8,128)S(1)}, s32[]{:S(2)}) async-start(f32[1,4,256,1024]{2,3,1,0:T(8,128)} %copy-done.2), calls=%async_computation.2 | async-start | bytes 6291456 | tf_op jit(solution)/shard_map/slice | solution.py:91
  111.5 25.8 %collective-permute-start.2 = (f32[1,1,1,256,1024]{3,4,2,1,0:T(8,128)}, f32[1,1,1,256,1024]{3,4,2,1,0:T(8,128)}, u32[]{:S(2)}, u32[]{:S(2)}) collective-permute-start(f32[1,1,1,256,1024]{3,4,2,1,0:T(8,128)} %slice_bitcast_fusion.5), channel_id=1, source_target_pairs={{0,1},{1,2},{2,3},{3,0},{4,5},{5,6},{6,7},{7,4},{8,9},{9,10},{10,1... | collective-permute-start | bytes 3145736 | tf_op jit(solution)/shard_map/ppermute | solution.py:21
  111.5 28.5 %collective-permute-start.4 = (f32[1,1,1,256,1024]{3,4,2,1,0:T(8,128)}, f32[1,1,1,256,1024]{3,4,2,1,0:T(8,128)}, u32[]{:S(2)}, u32[]{:S(2)}) collective-permute-start(f32[1,1,1,256,1024]{3,4,2,1,0:T(8,128)} %slice_bitcast_fusion.5), channel_id=1, source_target_pairs={{0,3},{1,0},{2,1},{3,2},{4,7},{5,4},{6,5},{7,6},{8,11},{9,8},{10,9... | collective-permute-start | bytes 3145736 | tf_op jit(solution)/shard_map/ppermute | solution.py:23
  137.3 25.0 %collective-permute-start.3 = (f32[1,1,1,256,1024]{3,4,2,1,0:T(8,128)}, f32[1,1,1,256,1024]{3,4,2,1,0:T(8,128)}, u32[]{:S(2)}, u32[]{:S(2)}) collective-permute-start(f32[1,1,1,256,1024]{3,4,2,1,0:T(8,128)} %collective-permute-done.2), channel_id=1, source_target_pairs={{0,1},{1,2},{2,3},{3,0},{4,5},{5,6},{6,7},{7,4},{8,9},{9,10},{10,1... | collective-permute-start | bytes 3145736 | tf_op jit(solution)/shard_map/ppermute | solution.py:21
  188.6 1.9 copy-start.10
  394.2 116.2 %copy-start.9 = (f32[1,3,256,1024]{3,2,1,0:T(8,128)S(1)}, f32[1,3,256,1024]{3,2,1,0:T(8,128)}, u32[]{:S(2)}) copy-start(f32[1,3,256,1024]{3,2,1,0:T(8,128)} %copy.147) | copy-start | bytes 9437188
  510.4 6.9 copy-start.14
  545.8 760.1 %all-gather.5.cloned.1.call-start = ((), (), s32[]{:S(2)}) async-start(), calls=%async_computation.1 | async-start | bytes 7864320 | tf_op jit(solution)/shard_map/all_gather | solution.py:96
  546.0 83.9 %collective-permute-start.6 = (bf16[1,4,256,256]{2,3,1,0:T(8,128)(2,1)S(1)}, bf16[1,4,256,256]{2,3,1,0:T(8,128)(2,1)S(1)}, u32[]{:S(2)}, u32[]{:S(2)}) collective-permute-start(bf16[1,4,256,256]{2,3,1,0:T(8,128)(2,1)S(1)} %bitcast.951), channel_id=1, source_target_pairs={{0,4},{4,0},{8,12},{12,8},{16,20},{20,16},{24,28},{28,24},{32,36},... | collective-permute-start | bytes 1572872 | tf_op jit(solution)/shard_map/ppermute | solution.py:31
  614.6 5.5 copy-start.12
  627.7 102.9 %collective-permute-start.5 = (bf16[1,768,3072]{2,1,0:T(8,128)(2,1)}, bf16[1,768,3072]{2,1,0:T(8,128)(2,1)}, u32[]{:S(2)}, u32[]{:S(2)}) collective-permute-start(bf16[1,768,3072]{2,1,0:T(8,128)(2,1)} %bitcast.954), channel_id=1, source_target_pairs={{0,8},{4,12},{8,0},{12,4},{16,24},{20,28},{24,16},{28,20},{32,40},... | collective-permute-start | bytes 14155784 | tf_op jit(solution)/shard_map/ppermute | solution.py:31
  631.3 165.1 %collective-permute-start.7 = (bf16[1,4,256,512]{2,3,1,0:T(8,128)(2,1)}, bf16[1,4,256,512]{2,3,1,0:T(8,128)(2,1)}, u32[]{:S(2)}, u32[]{:S(2)}) collective-permute-start(bf16[1,4,256,512]{2,3,1,0:T(8,128)(2,1)} %maximum_select_fusion.3), channel_id=1, source_target_pairs={{0,8},{4,12},{8,0},{12,4},{16,24},{20,28},{24,16},{28,20},{32,40},... | collective-permute-start | bytes 3145736 | tf_op jit(solution)/shard_map/ppermute | solution.py:31
  799.9 1.9 copy-start.3
  802.9 23.6 %slice-start.1 = ((f32[1,4,256,1024]{2,3,1,0:T(8,128)}), f32[1,3,256,1024]{2,3,1,0:T(8,128)S(1)}, s32[]{:S(2)}) async-start(f32[1,4,256,1024]{2,3,1,0:T(8,128)} %copy-done.3), calls=%async_computation.3 | async-start | bytes 6291456 | tf_op jit(solution)/shard_map/slice | solution.py:91
  802.9 23.5 %collective-permute-start.8 = (f32[1,1,1,256,1024]{3,4,2,1,0:T(8,128)}, f32[1,1,1,256,1024]{3,4,2,1,0:T(8,128)}, u32[]{:S(2)}, u32[]{:S(2)}) collective-permute-start(f32[1,1,1,256,1024]{3,4,2,1,0:T(8,128)} %slice_bitcast_fusion.2), channel_id=1, source_target_pairs={{0,1},{1,2},{2,3},{3,0},{4,5},{5,6},{6,7},{7,4},{8,9},{9,10},{10,1... | collective-permute-start | bytes 3145736 | tf_op jit(solution)/shard_map/ppermute | solution.py:21
  804.0 24.9 %collective-permute-start.10 = (f32[1,1,1,256,1024]{3,4,2,1,0:T(8,128)}, f32[1,1,1,256,1024]{3,4,2,1,0:T(8,128)}, u32[]{:S(2)}, u32[]{:S(2)}) collective-permute-start(f32[1,1,1,256,1024]{3,4,2,1,0:T(8,128)} %slice_bitcast_fusion.2), channel_id=1, source_target_pairs={{0,3},{1,0},{2,1},{3,2},{4,7},{5,4},{6,5},{7,6},{8,11},{9,8},{10,9... | collective-permute-start | bytes 3145736 | tf_op jit(solution)/shard_map/ppermute | solution.py:23
  826.5 22.5 %collective-permute-start.9 = (f32[1,1,1,256,1024]{3,4,2,1,0:T(8,128)}, f32[1,1,1,256,1024]{3,4,2,1,0:T(8,128)}, u32[]{:S(2)}, u32[]{:S(2)}) collective-permute-start(f32[1,1,1,256,1024]{3,4,2,1,0:T(8,128)} %collective-permute-done.8), channel_id=1, source_target_pairs={{0,1},{1,2},{2,3},{3,0},{4,5},{5,6},{6,7},{7,4},{8,9},{9,10},{10,1... | collective-permute-start | bytes 3145736 | tf_op jit(solution)/shard_map/ppermute | solution.py:21
  875.0 1.9 copy-start.11
  1080.9 115.9 %copy-start.8 = (f32[1,3,256,1024]{3,2,1,0:T(8,128)S(1)}, f32[1,3,256,1024]{3,2,1,0:T(8,128)}, u32[]{:S(2)}) copy-start(f32[1,3,256,1024]{3,2,1,0:T(8,128)} %copy.165) | copy-start | bytes 9437188
  1196.8 6.9 copy-start.15
  1230.5 4.1 copy-start.5
  1249.4 10.5 copy-start.7
  1265.9 43.5 %copy-start.13 = (bf16[1,768,1024]{1,2,0:T(8,128)(2,1)S(1)}, bf16[1,768,1024]{1,2,0:T(8,128)(2,1)}, u32[]{:S(2)}) copy-start(bf16[1,768,1024]{1,2,0:T(8,128)(2,1)} %convert_element_type.105) | copy-start | bytes 4718596
  1309.4 8.3 copy-start.1
  (3 other events, 5.3 us)
Sparse Core Ops, SparseCore 0:
  545.9 68.6 all-gather.2
  1234.7 71.1 all-gather.4
